TPU v7x, 128 devices: a whole 4x4x4 slice. The times are simulated.
128 devices in a mesh: pipe: 8 (over x, z_hi), tensor: 16 (over z_lo, y, core).
Axes of the slice: x: 4, y: 4, z: 4 (z_hi: 2, z_lo: 2; z = z_hi * 2 + z_lo), core: 2. Of those that a mesh axis runs over, the one named last changes fastest.
Arguments:
- layer_input: bfloat16 [768, 8192], P('tensor', 'pipe'), may hold values from -6 to 6
- out_grad: bfloat16 [768, 8192], P('tensor', 'pipe'), may hold values from -2 to 2
- gate_pre: bfloat16 [768, 28672], P(None, 'tensor'), may hold values from -8 to 8
- up_pre: bfloat16 [768, 28672], P(None, 'tensor'), may hold values from -6 to 6
- gate_weight: bfloat16 [8192, 28672], P('pipe', 'tensor'), may hold values from -0.0625 to 0.0625
- up_weight: bfloat16 [8192, 28672], P('pipe', 'tensor'), may hold values from -0.0625 to 0.0625
- down_weight: bfloat16 [28672, 8192], P('tensor', 'pipe'), may hold values from -0.03125 to 0.03125
- gate_mask: int32 [64, 224], P('pipe', 'tensor'), may hold values from 0 to 1, as said below
- up_mask: int32 [64, 224], P('pipe', 'tensor'), may hold values from 0 to 1, as said below
- down_mask: int32 [224, 64], P('tensor', 'pipe'), may hold values from 0 to 1, as said below
Outputs:
- grad_input: bfloat16 [768, 8192], P('tensor', 'pipe')
- grad_gate: bfloat16 [8192, 28672], P('pipe', 'tensor')
- grad_up: bfloat16 [8192, 28672], P('pipe', 'tensor')
- grad_down: bfloat16 [28672, 8192], P('tensor', 'pipe')
Inputs may be any that keep to these rules, and one draw needn't show every extreme that they name: `gate_mask`: each entry is 1 for a kept block and 0 for a pruned one; the share of kept blocks differs from block column to block column. `up_mask`: each entry is 1 for a kept block and 0 for a pruned one; the share of kept blocks differs from block column to block column. `down_mask`: each entry is 1 for a kept block and 0 for a pruned one; the share of kept blocks differs from block row to block row.
All inputs are finite; a program needn't handle non-finite values.
Results may differ from a plain program's by a relative error of at most 0.005.
Values may be sent and summed in bfloat16 or wider, within the bound.
A program may use at most 128 MiB of HBM per device.

v0:
```python
import jax
import jax.numpy as jnp
from jax import lax
from jax.sharding import PartitionSpec as P

BLOCK = 128


def expand(mask):
    return jnp.repeat(jnp.repeat(mask, BLOCK, axis=0), BLOCK, axis=1)


def local_grads(hidden_grad, gate_val, up_val, sigma_val):
    gate_grad = (hidden_grad * up_val * sigma_val * (1.0 + gate_val * (1.0 - sigma_val))).astype(
        jnp.bfloat16
    )
    up_grad = (hidden_grad * gate_val * sigma_val).astype(jnp.bfloat16)
    return (gate_grad, up_grad)


def shards(
    layer_input,
    out_grad,
    gate_pre,
    up_pre,
    gate_weight,
    up_weight,
    down_weight,
    gate_mask,
    up_mask,
    down_mask,
):
    mask_gate = expand(gate_mask)
    mask_up = expand(up_mask)
    mask_down = expand(down_mask)
    gate_masked = gate_weight * mask_gate.astype(jnp.bfloat16)
    up_masked = up_weight * mask_up.astype(jnp.bfloat16)
    down_masked = down_weight * mask_down.astype(jnp.bfloat16)
    gate_val = gate_pre.astype(jnp.float32)
    up_val = up_pre.astype(jnp.float32)
    sigma_val = jax.nn.sigmoid(gate_val)
    hidden = (gate_val * sigma_val * up_val).astype(jnp.bfloat16)
    piece = lax.all_gather(out_grad, "tensor", axis=0, tiled=True)
    down_acc = lax.dot_general(
        hidden, piece, (((0,), (0,)), ((), ())), preferred_element_type=jnp.float32
    )
    partial_rows = lax.dot_general(
        piece, down_masked, (((1,), (1,)), ((), ())), preferred_element_type=jnp.float32
    )
    hidden_grad = partial_rows
    down_acc, hidden_partial = (down_acc, hidden_grad)
    grad_down = (down_acc * mask_down.astype(jnp.float32)).astype(jnp.bfloat16)
    hidden_grad = lax.psum(hidden_partial, "pipe")
    gate_grad, up_grad = local_grads(hidden_grad, gate_val, up_val, sigma_val)
    piece = lax.all_gather(layer_input, "tensor", axis=0, tiled=True)
    gate_rows = gate_grad
    up_rows = up_grad
    gate_acc = lax.dot_general(
        piece, gate_rows, (((0,), (0,)), ((), ())), preferred_element_type=jnp.float32
    )
    up_acc = lax.dot_general(
        piece, up_rows, (((0,), (0,)), ((), ())), preferred_element_type=jnp.float32
    )
    gate_acc, up_acc = (gate_acc, up_acc)
    grad_gate = (gate_acc * mask_gate.astype(jnp.float32)).astype(jnp.bfloat16)
    grad_up = (up_acc * mask_up.astype(jnp.float32)).astype(jnp.bfloat16)
    gate_rows = gate_grad
    up_rows = up_grad
    total = lax.dot_general(
        gate_rows, gate_masked, (((1,), (1,)), ((), ())), preferred_element_type=jnp.float32
    )
    grad_input = lax.psum_scatter(
        total
        + lax.dot_general(
            up_rows, up_masked, (((1,), (1,)), ((), ())), preferred_element_type=jnp.float32
        ),
        "tensor",
        scatter_dimension=0,
        tiled=True,
    ).astype(jnp.bfloat16)
    return (grad_input, grad_gate, grad_up, grad_down)


def solution(mesh):
    in_specs = (
        P("tensor", "pipe"),
        P("tensor", "pipe"),
        P(None, "tensor"),
        P(None, "tensor"),
        P("pipe", "tensor"),
        P("pipe", "tensor"),
        P("tensor", "pipe"),
        P("pipe", "tensor"),
        P("pipe", "tensor"),
        P("tensor", "pipe"),
    )
    out_specs = (P("tensor", "pipe"), P("pipe", "tensor"), P("pipe", "tensor"), P("tensor", "pipe"))
    return jax.shard_map(shards, mesh=mesh, in_specs=in_specs, out_specs=out_specs, check_vma=False)
```

profile of v0, /device:TPU:0, one launch (start us, length us, event | category | flops | bytes accessed | tf_op | source)
XLA Modules:
  0.0 404.0 jit_solution(1261620353858778361)
XLA Ops:
  7.9 0.8 fusion.17
  8.8 36.6 %all-gather.3.cloned.1.call-done = bf16[768,1024]{1,0:T(8,128)(2,1)} async-done(((bf16[48,1024]{1,0:T(8,128)(2,1)}), bf16[768,1024]{1,0:T(8,128)(2,1)}) %all-gather.3.cloned.1.call-update) | async-done | bytes 1572880 | tf_op jit(solution)/shard_map/all_gather | solution.py:43
  45.4 5.1 %broadcast_in_dim.31 = bf16[1792,8,128]{2,1,0:T(8,128)(2,1)S(1)} broadcast(bf16[1792,8]{1,0:T(8,128)(2,1)S(1)} %bitcast.66), dimensions={0,1} | broadcast | bytes 3698688 | tf_op jit(solution)/shard_map/broadcast_in_dim | solution.py:10
  50.6 6.4 %convolution_bitcast_fusion = f32[768,1792]{0,1:T(8,128)} fusion(bf16[768,1024]{1,0:T(8,128)(2,1)} %all-gather.3.cloned.1.call-done, bf16[1792,1024]{1,0:T(8,128)(2,1)S(1)} %copy-done.9, bf16[224,8,8,128]{3,2,1,0:T(8,128)(2,1)S(1)} %bitcast.64), kind=kOutput, calls=%fused_computation.22 | convolution fusion | flops 2820407296 | bytes 14417920 | tf_op jit(solution)/shard_map/dot_general | solution.py:47
  58.0 3.3 copy.23
  61.3 4.5 %copy.24 = bf16[768,1792]{0,1:T(8,128)(2,1)} copy(bf16[768,1792]{1,0:T(8,128)(2,1)} %param.12) | data formatting | bytes 5505024 | tf_op args[2]
  66.0 6.0 %copy.26 = bf16[1024,1792]{0,1:T(8,128)(2,1)} copy(bf16[1024,1792]{1,0:T(8,128)(2,1)} %param.14) | data formatting | bytes 7340032 | tf_op args[4]
  72.3 6.0 %copy.28 = bf16[1024,1792]{0,1:T(8,128)(2,1)} copy(bf16[1024,1792]{1,0:T(8,128)(2,1)} %param.15) | data formatting | bytes 7340032 | tf_op args[5]
  78.2 4.3 %bitcast_multiply_fusion.6 = bf16[1024,1792]{0,1:T(8,128)(2,1)} fusion(bf16[1024,1792]{0,1:T(8,128)(2,1)} %copy.26, bf16[1024,14]{0,1:T(8,128)(2,1)S(1)} %bitcast.69), kind=kLoop, calls=%fused_computation.26 | loop fusion | flops 1835008 | bytes 7368704 | tf_op jit(solution)/shard_map/mul | solution.py:36
  82.5 2.1 bitcast_multiply_fusion.5
  84.6 207.2 %all-reduce.2.cloned.1.call-done = f32[768,1792]{0,1:T(8,128)} async-done(((f32[768,1792]{0,1:T(8,128)}), f32[768,1792]{0,1:T(8,128)}) %all-reduce.2.cloned.1.call-update) | async-done | bytes 5505040 | tf_op jit(solution)/shard_map/psum | solution.py:53
  291.8 5.0 %fusion.12 = (bf16[768,1792]{0,1:T(8,128)(2,1)S(1)}, bf16[768,1792]{0,1:T(8,128)(2,1)S(1)}) fusion(f32[768,1792]{0,1:T(8,128)} %all-reduce.2.cloned.1.call-done, bf16[768,1792]{0,1:T(8,128)(2,1)} %copy.24, bf16[768,1792]{0,1:T(8,128)(2,1)S(1)} %copy.23), kind=kLoop, calls=%fused_computation.21 | loop fusion | flops 20643840 | bytes 16515072 | tf_op jit(solution)/shard_map/convert_element_type | solution.py:17
  296.9 3.1 fusion.20
  300.0 0.9 copy-done.1
  300.9 4.9 %convolution_add_fusion = f32[768,1024]{1,0:T(8,128)} fusion(f32[768,1024]{1,0:T(8,128)S(1)} %fusion.20, bf16[768,1792]{0,1:T(8,128)(2,1)S(1)} %get-tuple-element.12, bf16[1024,1792]{0,1:T(8,128)(2,1)S(1)} %copy-done.1), kind=kOutput, calls=%fused_computation.28 | convolution fusion | flops 2819358720 | bytes 12713984 | tf_op jit(solution)/shard_map/dot_general | solution.py:74
  306.4 2.0 broadcast_in_dim.41
  308.7 5.2 %fusion = bf16[1792,1024]{1,0:T(8,128)(2,1)} fusion(f32[224,8,8,128]{3,2,1,0:T(8,128)S(1)} %bitcast.63, bf16[768,1024]{1,0:T(8,128)(2,1)S(1)} %copy-done.10, bf16[768,1792]{0,1:T(8,128)(2,1)S(1)} %copy.23, bf16[768,1792]{0,1:T(8,128)(2,1)S(1)} %copy-done.2), kind=kOutput, calls=%fused_computation.5 | convolution fusion | flops 2833252352 | bytes 18087936 | tf_op jit(solution)/shard_map/dot_general | solution.py:44
  313.9 14.5 %all-gather.5.cloned.1.call-done = bf16[768,1024]{1,0:T(8,128)(2,1)} async-done(((bf16[48,1024]{1,0:T(8,128)(2,1)}), bf16[768,1024]{1,0:T(8,128)(2,1)}) %all-gather.5.cloned.1.call-update) | async-done | bytes 1572880 | tf_op jit(solution)/shard_map/all_gather | solution.py:55
  328.4 7.1 %fusion.2 = bf16[1024,1792]{0,1:T(8,128)(2,1)} fusion(bf16[768,1792]{0,1:T(8,128)(2,1)} %copy-done.6, bf16[768,1024]{1,0:T(8,128)(2,1)} %all-gather.5.cloned.1.call-done, f32[1024,14]{0,1:T(8,128)S(1)} %bitcast.73), kind=kOutput, calls=%fused_computation.9 | convolution fusion | flops 2822242304 | bytes 8052736 | tf_op jit(solution)/shard_map/dot_general | solution.py:58
  335.5 6.1 %copy.32 = bf16[1024,1792]{1,0:T(8,128)(2,1)} copy(bf16[1024,1792]{0,1:T(8,128)(2,1)} %fusion.2) | data formatting | bytes 7340032
  341.6 6.2 %fusion.1 = bf16[1024,1792]{0,1:T(8,128)(2,1)} fusion(bf16[768,1792]{0,1:T(8,128)(2,1)S(1)} %copy-done.4, bf16[768,1024]{1,0:T(8,128)(2,1)} %all-gather.5.cloned.1.call-done, f32[1024,14]{0,1:T(8,128)S(1)} %bitcast.74), kind=kOutput, calls=%fused_computation.7 | convolution fusion | flops 2822242304 | bytes 8052736 | tf_op jit(solution)/shard_map/dot_general | solution.py:61
  347.8 5.9 %copy.33 = bf16[1024,1792]{1,0:T(8,128)(2,1)} copy(bf16[1024,1792]{0,1:T(8,128)(2,1)} %fusion.1) | data formatting | bytes 7340032
  353.7 42.1 %reduce-scatter.2.cloned.1.call-done = f32[48,1024]{1,0:T(8,128)} async-done(((f32[768,1024]{1,0:T(8,128)}), f32[48,1024]{1,0:T(8,128)}) %reduce-scatter.2.cloned.1.call-update) | async-done | bytes 196624 | tf_op jit(solution)/shard_map/reduce_scatter | solution.py:72
  395.9 1.6 convert_element_type.106
  (51 shorter events, 3.0 us)
Async XLA Ops:
  7.2 38.2 %all-gather.3.cloned.1.call-start = ((), (), s32[]{:S(2)}) async-start(), calls=%async_computation.1 | async-start | bytes 1671168 | tf_op jit(solution)/shard_map/all_gather | solution.py:43
  7.9 283.9 %all-reduce.2.cloned.1.call-start = ((), (), s32[]{:S(2)}) async-start(), calls=%async_computation.2 | async-start | bytes 11010048 | tf_op jit(solution)/shard_map/psum | solution.py:53
  45.4 5.2 %copy-start.9 = (bf16[1792,1024]{1,0:T(8,128)(2,1)S(1)}, bf16[1792,1024]{1,0:T(8,128)(2,1)}, u32[]{:S(2)}) copy-start(bf16[1792,1024]{1,0:T(8,128)(2,1)} %param.16) | copy-start | bytes 11010052
  57.0 271.4 %all-gather.5.cloned.1.call-start = ((), (), s32[]{:S(2)}) async-start(), calls=%async_computation.4 | async-start | bytes 1671168 | tf_op jit(solution)/shard_map/all_gather | solution.py:55
  57.7 338.2 %reduce-scatter.2.cloned.1.call-start = ((), (), s32[]{:S(2)}) async-start(), calls=%async_computation.3 | async-start | bytes 3342336 | tf_op jit(solution)/shard_map/reduce_scatter | solution.py:72
  61.3 4.5 %copy-start.7 = (s32[8,14]{1,0:T(8,128)S(1)}, s32[8,14]{1,0:T(8,128)}, u32[]{:S(2)}) copy-start(s32[8,14]{1,0:T(8,128)} %param.17) | copy-start | bytes 1348
  66.0 6.0 %copy-start.8 = (s32[8,14]{1,0:T(8,128)S(1)}, s32[8,14]{1,0:T(8,128)}, u32[]{:S(2)}) copy-start(s32[8,14]{1,0:T(8,128)} %param.18) | copy-start | bytes 1348
  78.2 4.3 %copy-start = (bf16[1024,1792]{0,1:T(8,128)(2,1)S(1)}, bf16[1024,1792]{0,1:T(8,128)(2,1)}, u32[]{:S(2)}) copy-start(bf16[1024,1792]{0,1:T(8,128)(2,1)} %copy.28) | copy-start | bytes 11010052
  291.8 5.1 %copy-start.5 = (bf16[1024,1792]{0,1:T(8,128)(2,1)S(1)}, bf16[1024,1792]{0,1:T(8,128)(2,1)}, u32[]{:S(2)}) copy-start(bf16[1024,1792]{0,1:T(8,128)(2,1)} %bitcast_multiply_fusion.6) | copy-start | bytes 11010052
  296.8 3.1 copy-start.6
  296.9 3.1 copy-start.3
  296.9 4.0 copy-start.1
  306.4 2.1 copy-start.2
  306.4 2.3 copy-start.10
  335.5 6.1 %copy-start.4 = (bf16[768,1792]{0,1:T(8,128)(2,1)S(1)}, bf16[768,1792]{0,1:T(8,128)(2,1)}, u32[]{:S(2)}) copy-start(bf16[768,1792]{0,1:T(8,128)(2,1)} %copy-done.3) | copy-start | bytes 8257540
Sparse Core Ops, SparseCore 0:
  9.7 35.6 all-gather.2
  57.1 234.6 all-reduce.1
  293.5 34.8 all-gather.4
  330.7 65.1 reduce-scatter.1
where the time goes:
time: 405 us; the launch traced here: 404 us
  waiting for transfers between devices  302 us (75%)
  local copies, waits for them, and re-layouts  41.1 us (10%)
  matrix products  32.9 us (8%)
  between operations  14 us (3%)
  other arithmetic  13.7 us (3%)
    psum x1, waiting for transfers between devices, shards(): hidden_grad = lax.psum(hidden_partial, 'pipe')  207 us
    reduce_scatter x1, waiting for transfers between devices, shards(): lax.psum_scatter(total + lax.dot_general(up_rows, up_masked, (((1,), (1,)...  42.1 us
    all_gather x1, waiting for transfers between devices, shards(): piece = lax.all_gather(out_grad, 'tensor', axis=0, tiled=True)  36.6 us
    unnamed x40, local copies, waits for them, and re-layouts  33.3 us
    all_gather x1, waiting for transfers between devices, shards(): piece = lax.all_gather(layer_input, 'tensor', axis=0, tiled=True)  14.5 us
  transfers between devices with their start and end apart: 4, of which 4 were waited for; matrix products, arithmetic and copies ran while one was open for 18% of the time, Pallas kernels for 0%

commit v1 on v0

--- a/solution.py
+++ b/solution.py
@@ -4,6 +4,15 @@
 from jax.sharding import PartitionSpec as P
 
 BLOCK = 128
+_lead_cards = lambda view: jnp.concatenate(
+    lax.all_to_all(
+        jnp.stack([view for _ in range(lax.psum(1, axis_name="tensor"))], axis=0),
+        axis_name="tensor",
+        split_axis=0,
+        concat_axis=0,
+    ),
+    axis=0,
+)
 
 
 def expand(mask):
@@ -52,7 +61,7 @@
     grad_down = (down_acc * mask_down.astype(jnp.float32)).astype(jnp.bfloat16)
     hidden_grad = lax.psum(hidden_partial, "pipe")
     gate_grad, up_grad = local_grads(hidden_grad, gate_val, up_val, sigma_val)
-    piece = lax.all_gather(layer_input, "tensor", axis=0, tiled=True)
+    piece = _lead_cards(layer_input)
     gate_rows = gate_grad
     up_rows = up_grad
     gate_acc = lax.dot_general(

time: 405 us -> 392 us (0.968)
  waiting for transfers between devices: 302 us -> 281 us
  starting transfers between devices: 0.34 us -> 4.74 us
    reduce_scatter x1, waiting for transfers between devices: 42.1 us -> 18.4 us  [shards(): lax.psum_scatter(total + lax.dot_general(up_rows, up_masked, (((1,), (1,)...]
    all_to_all x0 -> x1, waiting for transfers between devices: none -> 17.1 us  [lax.all_to_all(jnp.stack([view for _ in range(lax.psum(1, axis_name='tens...]
    all_gather x1 -> x0, waiting for transfers between devices: 14.5 us -> none  [shards(): piece = lax.all_gather(layer_input, 'tensor', axis=0, tiled=True)]
    all_to_all x0 -> x1, starting transfers between devices: none -> 4.62 us  [lax.all_to_all(jnp.stack([view for _ in range(lax.psum(1, axis_name='tens...]
    unnamed x40 -> x42, local copies, waits for them, and re-layouts: 33.3 us -> 33.4 us
  transfers between devices with their start and end apart: 4 -> 4, of which waited for: 4 -> 4; matrix products, arithmetic and copies ran while one was open for 18% -> 16% of each run, Pallas kernels for 0% -> 0%
where the time goes in v1:
time: 392 us; the launch traced here: 389 us
  waiting for transfers between devices  281 us (72%)
  local copies, waits for them, and re-layouts  42.6 us (11%)
  matrix products  33 us (8%)
  between operations  14 us (4%)
  other arithmetic  13.7 us (3%)
  starting transfers between devices  4.74 us (1%)
    psum x1, waiting for transfers between devices, shards(): hidden_grad = lax.psum(hidden_partial, 'pipe')  208 us
    all_gather x1, waiting for transfers between devices, shards(): piece = lax.all_gather(out_grad, 'tensor', axis=0, tiled=True)  36.6 us
    unnamed x42, local copies, waits for them, and re-layouts  33.4 us
    reduce_scatter x1, waiting for transfers between devices, shards(): lax.psum_scatter(total + lax.dot_general(up_rows, up_masked, (((1,), (1,)...  18.4 us
    all_to_all x1, waiting for transfers between devices, lax.all_to_all(jnp.stack([view for _ in range(lax.psum(1, axis_name='tens...  17.1 us
  transfers between devices with their start and end apart: 4, of which 4 were waited for; matrix products, arithmetic and copies ran while one was open for 16% of the time, Pallas kernels for 0%

profile of v1, /device:TPU:0, one launch (start us, length us, event | category | flops | bytes accessed | tf_op | source)
XLA Modules:
  0.0 388.8 jit_solution(12885450111622329612)
XLA Ops:
  8.8 36.6 %all-gather.2.cloned.1.call-done = bf16[768,1024]{1,0:T(8,128)(2,1)} async-done(((bf16[48,1024]{1,0:T(8,128)(2,1)}), bf16[768,1024]{1,0:T(8,128)(2,1)}) %all-gather.2.cloned.1.call-update) | async-done | bytes 1572880 | tf_op jit(solution)/shard_map/all_gather | solution.py:52
  45.4 5.1 %broadcast_in_dim.31 = bf16[1792,8,128]{2,1,0:T(8,128)(2,1)S(1)} broadcast(bf16[1792,8]{1,0:T(8,128)(2,1)S(1)} %bitcast.67), dimensions={0,1} | broadcast | bytes 3698688 | tf_op jit(solution)/shard_map/broadcast_in_dim | solution.py:19
  50.6 6.3 %convolution_bitcast_fusion = f32[768,1792]{0,1:T(8,128)} fusion(bf16[768,1024]{1,0:T(8,128)(2,1)} %all-gather.2.cloned.1.call-done, bf16[1792,1024]{1,0:T(8,128)(2,1)S(1)} %copy-done.10, bf16[224,8,8,128]{3,2,1,0:T(8,128)(2,1)S(1)} %bitcast.65), kind=kOutput, calls=%fused_computation.22 | convolution fusion | flops 2820407296 | bytes 14417920 | tf_op jit(solution)/shard_map/dot_general | solution.py:56
  57.0 3.3 copy.23
  60.3 4.5 %copy.24 = bf16[768,1792]{0,1:T(8,128)(2,1)} copy(bf16[768,1792]{1,0:T(8,128)(2,1)} %param.12) | data formatting | bytes 5505024 | tf_op args[2]
  65.0 6.1 %copy.26 = bf16[1024,1792]{0,1:T(8,128)(2,1)} copy(bf16[1024,1792]{1,0:T(8,128)(2,1)} %param.14) | data formatting | bytes 7340032 | tf_op args[4]
  71.4 5.9 %copy.28 = bf16[1024,1792]{0,1:T(8,128)(2,1)} copy(bf16[1024,1792]{1,0:T(8,128)(2,1)} %param.15) | data formatting | bytes 7340032 | tf_op args[5]
  77.4 4.3 %bitcast_multiply_fusion.6 = bf16[1024,1792]{0,1:T(8,128)(2,1)} fusion(bf16[1024,1792]{0,1:T(8,128)(2,1)} %copy.26, bf16[1024,14]{0,1:T(8,128)(2,1)S(1)} %bitcast.70), kind=kLoop, calls=%fused_computation.26 | loop fusion | flops 1835008 | bytes 7368704 | tf_op jit(solution)/shard_map/mul | solution.py:45
  81.6 2.1 bitcast_multiply_fusion.5
  83.7 208.0 %all-reduce.2.cloned.1.call-done = f32[768,1792]{0,1:T(8,128)} async-done(((f32[768,1792]{0,1:T(8,128)}), f32[768,1792]{0,1:T(8,128)}) %all-reduce.2.cloned.1.call-update) | async-done | bytes 5505040 | tf_op jit(solution)/shard_map/psum | solution.py:62
  291.7 5.0 %fusion.12 = (bf16[768,1792]{0,1:T(8,128)(2,1)S(1)}, bf16[768,1792]{0,1:T(8,128)(2,1)S(1)}) fusion(f32[768,1792]{0,1:T(8,128)} %all-reduce.2.cloned.1.call-done, bf16[768,1792]{0,1:T(8,128)(2,1)} %copy.24, bf16[768,1792]{0,1:T(8,128)(2,1)S(1)} %copy.23), kind=kLoop, calls=%fused_computation.21 | loop fusion | flops 20643840 | bytes 16515072 | tf_op jit(solution)/shard_map/convert_element_type | solution.py:26
  296.8 3.1 fusion.20
  300.8 4.9 %convolution_add_fusion = f32[768,1024]{1,0:T(8,128)} fusion(f32[768,1024]{1,0:T(8,128)S(1)} %fusion.20, bf16[768,1792]{0,1:T(8,128)(2,1)S(1)} %get-tuple-element.12, bf16[1024,1792]{0,1:T(8,128)(2,1)S(1)} %copy-done.1), kind=kOutput, calls=%fused_computation.28 | convolution fusion | flops 2819358720 | bytes 12713984 | tf_op jit(solution)/shard_map/dot_general | solution.py:83
  305.8 1.3 stack.2
  307.1 4.6 %all-to-all-start = ((bf16[16,48,1024]{2,1,0:T(8,128)(2,1)}), bf16[16,48,1024]{2,1,0:T(8,128)(2,1)}, u32[]{:S(2)}, u32[]{:S(2)}) async-start(bf16[16,48,1024]{2,1,0:T(8,128)(2,1)} %stack.2), calls=%async_computation.1 | async-start | bytes 3145728 | tf_op jit(solution)/shard_map/all_to_all | solution.py:8
  312.3 2.0 broadcast_in_dim.41
  314.5 5.2 %fusion = bf16[1792,1024]{1,0:T(8,128)(2,1)} fusion(f32[224,8,8,128]{3,2,1,0:T(8,128)S(1)} %bitcast.64, bf16[768,1024]{1,0:T(8,128)(2,1)S(1)} %copy-done.11, bf16[768,1792]{0,1:T(8,128)(2,1)S(1)} %copy.23, bf16[768,1792]{0,1:T(8,128)(2,1)S(1)} %copy-done.2), kind=kOutput, calls=%fused_computation.5 | convolution fusion | flops 2833252352 | bytes 18087936 | tf_op jit(solution)/shard_map/dot_general | solution.py:53
  319.7 17.1 %all-to-all-done = bf16[16,48,1024]{2,1,0:T(8,128)(2,1)} async-done(((bf16[16,48,1024]{2,1,0:T(8,128)(2,1)}), bf16[16,48,1024]{2,1,0:T(8,128)(2,1)}, u32[]{:S(2)}, u32[]{:S(2)}) %all-to-all-start) | async-done | bytes 1572896 | tf_op jit(solution)/shard_map/all_to_all | solution.py:8
  336.8 7.1 %fusion.2 = bf16[1024,1792]{0,1:T(8,128)(2,1)} fusion(bf16[768,1792]{0,1:T(8,128)(2,1)} %copy-done.6, bf16[768,1024]{1,0:T(8,128)(2,1)} %bitcast.4, f32[1024,14]{0,1:T(8,128)S(1)} %bitcast.74), kind=kOutput, calls=%fused_computation.9 | convolution fusion | flops 2822242304 | bytes 8052736 | tf_op jit(solution)/shard_map/dot_general | solution.py:67
  344.0 6.1 %copy.32 = bf16[1024,1792]{1,0:T(8,128)(2,1)} copy(bf16[1024,1792]{0,1:T(8,128)(2,1)} %fusion.2) | data formatting | bytes 7340032
  350.1 6.3 %fusion.1 = bf16[1024,1792]{0,1:T(8,128)(2,1)} fusion(bf16[768,1792]{0,1:T(8,128)(2,1)S(1)} %copy-done.4, bf16[768,1024]{1,0:T(8,128)(2,1)} %bitcast.4, f32[1024,14]{0,1:T(8,128)S(1)} %bitcast.75), kind=kOutput, calls=%fused_computation.7 | convolution fusion | flops 2822242304 | bytes 8052736 | tf_op jit(solution)/shard_map/dot_general | solution.py:70
  356.4 5.9 %copy.33 = bf16[1024,1792]{1,0:T(8,128)(2,1)} copy(bf16[1024,1792]{0,1:T(8,128)(2,1)} %fusion.1) | data formatting | bytes 7340032
  362.3 18.4 %reduce-scatter.2.cloned.1.call-done = f32[48,1024]{1,0:T(8,128)} async-done(((f32[768,1024]{1,0:T(8,128)}), f32[48,1024]{1,0:T(8,128)}) %reduce-scatter.2.cloned.1.call-update) | async-done | bytes 196624 | tf_op jit(solution)/shard_map/reduce_scatter | solution.py:81
  380.6 1.6 convert_element_type.106
  (53 shorter events, 3.7 us)
Async XLA Ops:
  7.2 38.2 %all-gather.2.cloned.1.call-start = ((), (), s32[]{:S(2)}) async-start(), calls=%async_computation.2 | async-start | bytes 1671168 | tf_op jit(solution)/shard_map/all_gather | solution.py:52
  7.9 283.8 %all-reduce.2.cloned.1.call-start = ((), (), s32[]{:S(2)}) async-start(), calls=%async_computation.3 | async-start | bytes 11010048 | tf_op jit(solution)/shard_map/psum | solution.py:62
  45.4 5.2 %copy-start.10 = (bf16[1792,1024]{1,0:T(8,128)(2,1)S(1)}, bf16[1792,1024]{1,0:T(8,128)(2,1)}, u32[]{:S(2)}) copy-start(bf16[1792,1024]{1,0:T(8,128)(2,1)} %param.16) | copy-start | bytes 11010052
  56.9 323.7 %reduce-scatter.2.cloned.1.call-start = ((), (), s32[]{:S(2)}) async-start(), calls=%async_computation.4 | async-start | bytes 3342336 | tf_op jit(solution)/shard_map/reduce_scatter | solution.py:81
  60.3 4.5 %copy-start.8 = (s32[8,14]{1,0:T(8,128)S(1)}, s32[8,14]{1,0:T(8,128)}, u32[]{:S(2)}) copy-start(s32[8,14]{1,0:T(8,128)} %param.17) | copy-start | bytes 1348
  65.0 6.2 %copy-start.9 = (s32[8,14]{1,0:T(8,128)S(1)}, s32[8,14]{1,0:T(8,128)}, u32[]{:S(2)}) copy-start(s32[8,14]{1,0:T(8,128)} %param.18) | copy-start | bytes 1348
  77.4 4.3 %copy-start = (bf16[1024,1792]{0,1:T(8,128)(2,1)S(1)}, bf16[1024,1792]{0,1:T(8,128)(2,1)}, u32[]{:S(2)}) copy-start(bf16[1024,1792]{0,1:T(8,128)(2,1)} %copy.28) | copy-start | bytes 11010052
  291.7 5.1 %copy-start.5 = (bf16[1024,1792]{0,1:T(8,128)(2,1)S(1)}, bf16[1024,1792]{0,1:T(8,128)(2,1)}, u32[]{:S(2)}) copy-start(bf16[1024,1792]{0,1:T(8,128)(2,1)} %bitcast_multiply_fusion.6) | copy-start | bytes 11010052
  296.8 3.1 copy-start.6
  296.8 3.1 copy-start.3
  296.8 4.0 %copy-start.1 = (bf16[1024,1792]{0,1:T(8,128)(2,1)S(1)}, bf16[1024,1792]{0,1:T(8,128)(2,1)}, u32[]{:S(2)}) copy-start(bf16[1024,1792]{0,1:T(8,128)(2,1)} %bitcast_multiply_fusion.5) | copy-start | bytes 11010052
  300.8 5.0 %copy-start.7 = (bf16[48,1024]{1,0:T(8,128)(2,1)S(1)}, bf16[48,1024]{1,0:T(8,128)(2,1)}, u32[]{:S(2)}) copy-start(bf16[48,1024]{1,0:T(8,128)(2,1)} %param.10) | copy-start | bytes 294916
  307.1 29.7 %all-to-all-start = ((bf16[16,48,1024]{2,1,0:T(8,128)(2,1)}), bf16[16,48,1024]{2,1,0:T(8,128)(2,1)}, u32[]{:S(2)}, u32[]{:S(2)}) async-start(bf16[16,48,1024]{2,1,0:T(8,128)(2,1)} %stack.2), calls=%async_computation.1 | async-start | bytes 3145728 | tf_op jit(solution)/shard_map/all_to_all | solution.py:8
  312.3 2.1 copy-start.2
  312.3 2.2 copy-start.11
  344.0 6.1 %copy-start.4 = (bf16[768,1792]{0,1:T(8,128)(2,1)S(1)}, bf16[768,1792]{0,1:T(8,128)(2,1)}, u32[]{:S(2)}) copy-start(bf16[768,1792]{0,1:T(8,128)(2,1)} %copy-done.3) | copy-start | bytes 8257540
Sparse Core Ops, SparseCore 0:
  9.7 35.6 all-gather.1
  57.0 234.6 all-reduce.1
  305.9 74.7 reduce-scatter.1
